TPU v7x, 32 devices: a whole 2x2x4 slice. The times are simulated.
32 devices in a mesh: dp: 4 (over y, x), expert: 8 (over z, core).
Axes of the slice: x: 2, y: 2, z: 4, core: 2. Of those that a mesh axis runs over, the one named last changes fastest.
Arguments:
- tokens: bfloat16 [32768, 768], P(('dp', 'expert')), may hold values from -6 to 6
- gain_one: float32 [768], replicated, may hold values from 0.25 to 1.75
- query_w: bfloat16 [768, 768], replicated, may hold values from -0.109375 to 0.109375
- key_w: bfloat16 [768, 768], replicated, may hold values from -0.109375 to 0.109375
- value_w: bfloat16 [768, 768], replicated, may hold values from -0.21875 to 0.21875
- out_w: bfloat16 [768, 768], replicated, may hold values from -0.625 to 0.625
- rel_table: float32 [32, 12], replicated, may hold values from -4 to 4
- gain_two: float32 [768], replicated, may hold values from 0.25 to 1.75
- router_w: bfloat16 [768, 8], replicated, may hold values from -0.15625 to 0.15625
- expert_in: bfloat16 [8, 768, 3072], P('expert'), may hold values from -0.21875 to 0.21875
- expert_out: bfloat16 [8, 3072, 768], P('expert'), may hold values from -0.875 to 0.875
- routes: int32 [32768, 1], P(('dp', 'expert')), may hold values from 0 to 7
- buckets: int32 [2047], replicated, may hold values from 0 to 31, as said below
- cotangent: bfloat16 [32768, 768], P(('dp', 'expert')), may hold values from -6 to 6
Outputs:
- output: bfloat16 [32768, 768], P(('dp', 'expert'))
- input_grad: float32 [32768, 768], P(('dp', 'expert'))
- query_grad: float32 [768, 768], replicated
- key_grad: float32 [768, 768], replicated
- value_grad: float32 [768, 768], replicated
- out_grad: float32 [768, 768], replicated
- rel_grad: float32 [32, 12], replicated
- gain_one_grad: float32 [768], replicated
- gain_two_grad: float32 [768], replicated
- router_grad: float32 [768, 8], replicated
- expert_in_grad: float32 [8, 768, 3072], P('expert', 'dp')
- expert_out_grad: float32 [8, 3072, 768], P('expert', None, 'dp')
Inputs may be any that keep to these rules, and one draw needn't show every extreme that they name: buckets depends only on the distance |j - i| and on the sign of j - i, never falls as the distance grows on either side, is below 16 for j - i <= 0 and 16 or more for j - i > 0.
All inputs are finite; a program needn't handle non-finite values.
Results may differ from a plain program's by a relative error of at most 0.015.
The roundings to bfloat16 on the way count: a program that leaves them out, or rounds other values in their place, can miss the bound.
Values may be sent and summed in bfloat16 or wider, within the bound.
A program may use at most 448 MiB of HBM per device.

v0:
```python
import jax
import jax.numpy as jnp
from jax import lax
from jax.sharding import PartitionSpec as P

epsilon = 1e-06
highest = lax.Precision.HIGHEST


def rms_forward(values, gain_vec):
    row_scale = lax.rsqrt(jnp.mean(values * values, axis=-1, keepdims=True) + epsilon)
    return (values * row_scale * gain_vec, row_scale)


def rms_backward(grad_norm, values, row_scale, gain_vec):
    weighted = grad_norm * gain_vec
    gain_grad = jnp.sum(grad_norm * values * row_scale, axis=0)
    grad_in = row_scale * weighted - values * row_scale**3 * jnp.mean(
        weighted * values, axis=-1, keepdims=True
    )
    return (grad_in, gain_grad)


def gelu_tanh(values):
    return jax.nn.gelu(values, approximate=True)


def window_start(row_start, block_rows, seq_len):
    return seq_len - row_start - block_rows


def bias_block(bias_heads, row_start, block_rows, seq_len):
    head_count = bias_heads.shape[0]
    width = seq_len + block_rows - 1
    first = window_start(row_start, block_rows, seq_len)
    window = bias_heads[:, first : first + width]
    flat = jnp.tile(window, (1, block_rows))
    flat = flat[:, block_rows - 1 : block_rows - 1 + block_rows * (width - 1)]
    return flat.reshape(head_count, block_rows, width - 1)[:, :, :seq_len]


def diagonal_sums(score_grad, block_rows, seq_len):
    head_count = score_grad.shape[0]
    width = seq_len + block_rows - 1
    padded = jnp.pad(score_grad, ((0, 0), (0, 0), (0, width - 1 - seq_len)))
    flat = padded.reshape(head_count, block_rows * (width - 1))
    flat = jnp.pad(flat, ((0, 0), (block_rows - 1, 1)))
    return jnp.sum(flat.reshape(head_count, block_rows, width), axis=1)


def project(left, right):
    return jnp.dot(left, right, preferred_element_type=jnp.float32)


def project_left(left, right):
    return jnp.einsum("td,te->de", left, right, preferred_element_type=jnp.float32)


def project_right(left, right):
    return jnp.einsum("te,de->td", left, right, preferred_element_type=jnp.float32)


def on_device(
    tokens,
    gain_one,
    query_w,
    key_w,
    value_w,
    out_w,
    rel_table,
    gain_two,
    router_w,
    expert_in,
    expert_out,
    routes,
    buckets,
    cotangent,
):
    seq_len, model_width = tokens.shape
    head_count = rel_table.shape[1]
    head_dim = model_width // head_count
    experts = lax.axis_size("expert")
    capacity = (5 * seq_len + 4 * experts - 1) // (4 * experts)
    block_rows = min(512, seq_len)
    block_count = seq_len // block_rows
    trash_slot = experts * capacity
    width = seq_len + block_rows - 1
    tokens_f = tokens.astype(jnp.float32)
    normed, scale_one = rms_forward(tokens_f, gain_one)
    normed_low = normed.astype(jnp.bfloat16)
    queries = project(normed_low, query_w).astype(jnp.bfloat16)
    key_rows = project(normed_low, key_w).astype(jnp.bfloat16)
    value_rows = project(normed_low, value_w).astype(jnp.bfloat16)
    query_heads = queries.reshape(seq_len, head_count, head_dim)
    key_heads = key_rows.reshape(seq_len, head_count, head_dim)
    value_heads = value_rows.reshape(seq_len, head_count, head_dim)
    bucket_hot = (
        buckets[:, None] == jnp.arange(rel_table.shape[0], dtype=jnp.int32)[None, :]
    ).astype(jnp.float32)
    bias_heads = jnp.einsum("lb,bh->hl", bucket_hot, rel_table, precision=highest)
    context_parts = []
    logsum_parts = []
    for block_idx in range(block_count):
        row_start = block_idx * block_rows
        bias_now = bias_block(bias_heads, row_start, block_rows, seq_len)
        query_blk = query_heads[row_start : row_start + block_rows]
        scores = (
            jnp.einsum("qhd,khd->hqk", query_blk, key_heads, preferred_element_type=jnp.float32)
            + bias_now
        )
        row_max = jnp.max(scores, axis=-1, keepdims=True)
        exp_scores = jnp.exp(scores - row_max)
        row_total = jnp.sum(exp_scores, axis=-1, keepdims=True)
        att_weights = (exp_scores / row_total).astype(jnp.bfloat16)
        context_parts.append(
            jnp.einsum(
                "hqk,khd->qhd", att_weights, value_heads, preferred_element_type=jnp.float32
            ).astype(jnp.bfloat16)
        )
        logsum_parts.append(row_max + jnp.log(row_total))
    context = jnp.concatenate(context_parts, axis=0).reshape(seq_len, model_width)
    hidden = tokens_f + project(context, out_w)
    normed_two, scale_two = rms_forward(hidden, gain_two)
    normed_two_low = normed_two.astype(jnp.bfloat16)
    router_probs = jax.nn.softmax(project(normed_two_low, router_w), axis=-1)
    route_ids = routes[:, 0]
    route_hot = (route_ids[:, None] == jnp.arange(experts, dtype=jnp.int32)[None, :]).astype(
        jnp.int32
    )
    route_float = route_hot.astype(jnp.float32)
    position = jnp.sum((jnp.cumsum(route_hot, axis=0) - 1) * route_hot, axis=1)
    slot_index = jnp.where(position < capacity, route_ids * capacity + position, trash_slot)
    gate_value = jnp.sum(router_probs * route_float, axis=-1)
    send_rows = (
        jnp.zeros((trash_slot + 1, model_width), jnp.bfloat16).at[slot_index].set(normed_two_low)
    )
    send_rows = send_rows[:trash_slot].reshape(experts, capacity, model_width)
    weight_in = expert_in[0]
    weight_out = expert_out[0]
    received = lax.all_to_all(send_rows, "expert", split_axis=0, concat_axis=0, tiled=True)
    preact = jnp.einsum("scd,df->scf", received, weight_in, preferred_element_type=jnp.float32)
    active = gelu_tanh(preact).astype(jnp.bfloat16)
    produced = jnp.einsum(
        "scf,fd->scd", active, weight_out, preferred_element_type=jnp.float32
    ).astype(jnp.bfloat16)
    results = (received, preact, produced)
    received = results[0]
    produced = results[-1]
    returned = lax.all_to_all(produced, "expert", split_axis=0, concat_axis=0, tiled=True)
    padded = jnp.concatenate(
        [returned.reshape(trash_slot, model_width), jnp.zeros((1, model_width), jnp.bfloat16)],
        axis=0,
    )
    gathered = padded[slot_index].astype(jnp.float32)
    output = (hidden + gate_value[:, None] * gathered).astype(jnp.bfloat16)
    grad_out = cotangent.astype(jnp.float32)
    grad_gather = (grad_out * gate_value[:, None]).astype(jnp.bfloat16)
    gate_grad = jnp.sum(grad_out * gathered, axis=-1)
    grad_send = (
        jnp.zeros((trash_slot + 1, model_width), jnp.bfloat16).at[slot_index].set(grad_gather)
    )
    grad_send = grad_send[:trash_slot].reshape(experts, capacity, model_width)
    grad_produced = lax.all_to_all(grad_send, "expert", split_axis=0, concat_axis=0, tiled=True)
    preact_kept = results[1]
    gelu_values, gelu_pullback = jax.vjp(gelu_tanh, preact_kept)
    active = gelu_values.astype(jnp.bfloat16)
    grad_active = jnp.einsum(
        "scd,fd->scf", grad_produced, weight_out, preferred_element_type=jnp.float32
    )
    grad_preact = gelu_pullback(grad_active)[0].astype(jnp.bfloat16)
    grad_received = jnp.einsum(
        "scf,df->scd", grad_preact, weight_in, preferred_element_type=jnp.float32
    ).astype(jnp.bfloat16)
    grad_rows = lax.all_to_all(grad_received, "expert", split_axis=0, concat_axis=0, tiled=True)
    in_grad = jnp.einsum("scd,scf->df", received, grad_preact, preferred_element_type=jnp.float32)
    out_grad_local = jnp.einsum(
        "scf,scd->fd", active, grad_produced, preferred_element_type=jnp.float32
    )
    in_share, out_share = (
        lax.psum_scatter(
            in_grad.astype(jnp.bfloat16), "dp", scatter_dimension=0, tiled=True
        ).astype(jnp.float32),
        lax.psum_scatter(
            out_grad_local.astype(jnp.bfloat16), "dp", scatter_dimension=1, tiled=True
        ).astype(jnp.float32),
    )
    grad_padded = jnp.concatenate(
        [grad_rows.reshape(trash_slot, model_width), jnp.zeros((1, model_width), jnp.bfloat16)],
        axis=0,
    )
    grad_dispatched = grad_padded[slot_index].astype(jnp.float32)
    logit_low = ((gate_grad * gate_value)[:, None] * (route_float - router_probs)).astype(
        jnp.bfloat16
    )
    router_grad = project_left(normed_two_low, logit_low)
    grad_normed_two = project_right(logit_low, router_w) + grad_dispatched
    grad_hidden_norm, gain_two_grad = rms_backward(grad_normed_two, hidden, scale_two, gain_two)
    grad_hidden = grad_out + grad_hidden_norm
    branch_low = grad_hidden.astype(jnp.bfloat16)
    out_w_grad = project_left(context, branch_low)
    grad_context = (
        project_right(branch_low, out_w).astype(jnp.bfloat16).reshape(seq_len, head_count, head_dim)
    )
    key_grad_sum = jnp.zeros((seq_len, head_count, head_dim), jnp.float32)
    value_grad_sum = jnp.zeros((seq_len, head_count, head_dim), jnp.float32)
    offset_grad = jnp.zeros((head_count, 2 * seq_len - 1), jnp.float32)
    query_parts = []
    for block_idx in range(block_count):
        row_start = block_idx * block_rows
        bias_now = bias_block(bias_heads, row_start, block_rows, seq_len)
        query_blk = query_heads[row_start : row_start + block_rows]
        grad_ctx_blk = grad_context[row_start : row_start + block_rows]
        scores = (
            jnp.einsum("qhd,khd->hqk", query_blk, key_heads, preferred_element_type=jnp.float32)
            + bias_now
        )
        att_probs = jnp.exp(scores - logsum_parts[block_idx])
        att_low = att_probs.astype(jnp.bfloat16)
        value_grad_sum = value_grad_sum + jnp.einsum(
            "hqk,qhd->khd", att_low, grad_ctx_blk, preferred_element_type=jnp.float32
        )
        prob_grad = jnp.einsum(
            "qhd,khd->hqk", grad_ctx_blk, value_heads, preferred_element_type=jnp.float32
        )
        score_grad = att_probs * (
            prob_grad - jnp.sum(att_probs * prob_grad, axis=-1, keepdims=True)
        )
        first = window_start(row_start, block_rows, seq_len)
        offset_grad = offset_grad.at[:, first : first + width].add(
            diagonal_sums(score_grad, block_rows, seq_len)
        )
        score_low = score_grad.astype(jnp.bfloat16)
        query_parts.append(
            jnp.einsum(
                "hqk,khd->qhd", score_low, key_heads, preferred_element_type=jnp.float32
            ).astype(jnp.bfloat16)
        )
        key_grad_sum = key_grad_sum + jnp.einsum(
            "hqk,qhd->khd", score_low, query_blk, preferred_element_type=jnp.float32
        )
    query_grad_low = jnp.concatenate(query_parts, axis=0).reshape(seq_len, model_width)
    key_grad_low = key_grad_sum.astype(jnp.bfloat16).reshape(seq_len, model_width)
    value_grad_low = value_grad_sum.astype(jnp.bfloat16).reshape(seq_len, model_width)
    query_w_grad = project_left(normed_low, query_grad_low)
    key_w_grad = project_left(normed_low, key_grad_low)
    value_w_grad = project_left(normed_low, value_grad_low)
    grad_normed = (
        project_right(query_grad_low, query_w)
        + project_right(key_grad_low, key_w)
        + project_right(value_grad_low, value_w)
    )
    grad_tokens_norm, gain_one_grad = rms_backward(grad_normed, tokens_f, scale_one, gain_one)
    input_grad = grad_hidden + grad_tokens_norm
    rel_grad = jnp.einsum("lb,hl->bh", bucket_hot, offset_grad, precision=highest)
    (
        query_w_grad,
        key_w_grad,
        value_w_grad,
        out_w_grad,
        rel_grad,
        gain_one_grad,
        gain_two_grad,
        router_grad,
    ) = lax.psum(
        (
            query_w_grad,
            key_w_grad,
            value_w_grad,
            out_w_grad,
            rel_grad,
            gain_one_grad,
            gain_two_grad,
            router_grad,
        ),
        ("dp", "expert"),
    )
    return (
        output,
        input_grad,
        query_w_grad,
        key_w_grad,
        value_w_grad,
        out_w_grad,
        rel_grad,
        gain_one_grad,
        gain_two_grad,
        router_grad,
        in_share[None],
        out_share[None],
    )


def solution(mesh):
    return jax.shard_map(
        on_device,
        mesh=mesh,
        in_specs=(
            P(("dp", "expert"), None),
            P(),
            P(),
            P(),
            P(),
            P(),
            P(),
            P(),
            P(),
            P("expert", None, None),
            P("expert", None, None),
            P(("dp", "expert"), None),
            P(),
            P(("dp", "expert"), None),
        ),
        out_specs=(
            P(("dp", "expert"), None),
            P(("dp", "expert"), None),
            P(),
            P(),
            P(),
            P(),
            P(),
            P(),
            P(),
            P(),
            P("expert", "dp", None),
            P("expert", None, "dp"),
        ),
        check_vma=False,
    )
```

profile of v0, /device:TPU:0, one launch (start us, length us, event | category | flops | bytes accessed | tf_op | source)
XLA Modules:
  0.0 1550.1 jit_solution(11302961146978953554)
XLA Ops:
  28.0 12.7 tile.8
  40.7 61.7 %tile.9 = f32[12,785920]{1,0:T(8,128)} reshape(f32[12,512,1535]{2,1,0:T(8,128)} %tile.8) | data formatting | bytes 75448320 | tf_op jit(solution)/shard_map/tile | solution.py:37
  102.5 38.2 %slice.122 = f32[12,785408]{1,0:T(8,128)} slice(f32[12,785920]{1,0:T(8,128)} %tile.9), slice={[0:12], [511:785919]} | slice | bytes 75399168 | tf_op jit(solution)/shard_map/slice | solution.py:38
  140.7 90.3 %reshape.233 = f32[12,512,1534]{2,1,0:T(8,128)} reshape(f32[12,785408]{1,0:T(8,128)} %slice.122) | data formatting | bytes 75399168 | tf_op jit(solution)/shard_map/reshape | solution.py:39
  231.1 12.8 tile.10
  243.8 61.5 %tile.11 = f32[12,785920]{1,0:T(8,128)} reshape(f32[12,512,1535]{2,1,0:T(8,128)} %tile.10) | data formatting | bytes 75448320 | tf_op jit(solution)/shard_map/tile | solution.py:37
  305.3 38.2 %slice.126 = f32[12,785408]{1,0:T(8,128)} slice(f32[12,785920]{1,0:T(8,128)} %tile.11), slice={[0:12], [511:785919]} | slice | bytes 75399168 | tf_op jit(solution)/shard_map/slice | solution.py:38
  343.6 86.1 %reshape.234 = f32[12,512,1534]{2,1,0:T(8,128)} reshape(f32[12,785408]{1,0:T(8,128)} %slice.126) | data formatting | bytes 75399168 | tf_op jit(solution)/shard_map/reshape | solution.py:39
  429.7 16.8 %fusion.105 = (f32[12,512]{1,0:T(8,128)}, f32[12,512,1024]{2,1,0:T(8,128)}) fusion(f32[12,512,1534]{2,1,0:T(8,128)} %reshape.233, bf16[512,12,64]{0,2,1:T(8,128)(2,1)S(1)} %bitcast.134, bf16[1024,12,64]{0,2,1:T(8,128)(2,1)S(1)} %bitcast.121), kind=kOutput, calls=%fused_computation.149 | convolution fusion | flops 817883136 | bytes 52715520 | tf_op jit(solution)/shard_map/qhd,khd->hqk/dot_general | solution.py:108
  469.0 16.9 %fusion.104 = (f32[12,512]{1,0:T(8,128)}, f32[12,512,1024]{2,1,0:T(8,128)}) fusion(f32[12,512,1534]{2,1,0:T(8,128)} %reshape.234, bf16[512,12,64]{0,2,1:T(8,128)(2,1)S(1)} %bitcast.128, bf16[1024,12,64]{0,2,1:T(8,128)(2,1)S(1)} %bitcast.122), kind=kOutput, calls=%fused_computation.148 | convolution fusion | flops 817883136 | bytes 52715520 | tf_op jit(solution)/shard_map/qhd,khd->hqk/dot_general | solution.py:108
  524.4 52.5 %all_to_all.20 = bf16[8,160,768]{2,1,0:T(8,128)(2,1)S(1)} all-to-all(bf16[8,160,768]{2,1,0:T(8,128)(2,1)S(1)} %bitcast.125), channel_id=1, replica_groups=mesh['dp'=4,'expert'=8] {'expert'}, dimensions={0} | all-to-all | bytes 3932160 | tf_op jit(solution)/shard_map/all_to_all | solution.py:140
  609.8 43.2 %all-to-all-done.1 = bf16[8,160,768]{2,1,0:T(8,128)(2,1)} async-done(((bf16[8,160,768]{2,1,0:T(8,128)(2,1)}), bf16[8,160,768]{2,1,0:T(8,128)(2,1)}, u32[]{:S(2)}, u32[]{:S(2)}) %all-to-all-start.1) | async-done | bytes 1966112 | tf_op jit(solution)/shard_map/all_to_all | solution.py:149
  675.0 48.8 %all_to_all.21 = bf16[8,160,768]{2,1,0:T(8,128)(2,1)S(1)} all-to-all(bf16[8,160,768]{2,1,0:T(8,128)(2,1)S(1)} %bitcast.127), channel_id=1, replica_groups=mesh['dp'=4,'expert'=8] {'expert'}, dimensions={0} | all-to-all | bytes 3932160 | tf_op jit(solution)/shard_map/all_to_all | solution.py:163
  735.9 17.6 %fusion.10 = bf16[8,160,3072]{2,1,0:T(8,128)(2,1)S(1)} fusion(f32[8,160,3072]{2,1,0:T(8,128)} %copy-done.68, bf16[8,160,768]{2,1,0:T(8,128)(2,1)S(1)} %all_to_all.21, bf16[1,3072,768]{2,1,0:T(8,128)(2,1)} %param.28), kind=kOutput, calls=%fused_computation.28 | convolution fusion | flops 6118440960 | bytes 30277632 | tf_op jit(solution)/shard_map/scd,fd->scf/dot_general | solution.py:167
  782.4 34.1 %all-to-all-done.3 = bf16[8,160,768]{2,1,0:T(8,128)(2,1)S(1)} async-done(((bf16[8,160,768]{2,1,0:T(8,128)(2,1)}), bf16[8,160,768]{2,1,0:T(8,128)(2,1)S(1)}, u32[]{:S(2)}, u32[]{:S(2)}) %all-to-all-start.3) | async-done | bytes 1966112 | tf_op jit(solution)/shard_map/all_to_all | solution.py:174
  837.1 20.3 %multiply_reduce_fusion.1 = (f32[12,512]{1,0:T(8,128)}, f32[12,512,1024]{2,1,0:T(8,128)}) fusion(f32[12,512,1024]{2,1,0:T(8,128)} %get-tuple-element.89, f32[12,512]{1,0:T(8,128)} %log_add_fusion.1, bf16[512,12,64]{0,2,1:T(8,128)(2,1)S(1)} %bitcast.130, bf16[1024,12,64]{0,2,1:T(8,128)(2,1)S(1)} %bitcast.139), kind=kOutput, calls=%fused_computation.10 | convolution fusion | flops 824174592 | bytes 52740096 | tf_op jit(solution)/shard_map/qhd,khd->hqk/dot_general | solution.py:222
  857.4 25.9 %subtract_multiply_fusion.1 = f32[12,512,1024]{2,1,0:T(8,128)} fusion(f32[12,512,1024]{2,1,0:T(8,128)} %get-tuple-element.98, f32[12,512,1024]{2,1,0:T(8,128)} %get-tuple-element.89, f32[12,512]{1,0:T(8,128)} %get-tuple-element.97, f32[12,512]{1,0:T(8,128)} %log_add_fusion.1), kind=kLoop, calls=%fused_computation.9 | loop fusion | flops 18874368 | bytes 75546624 | tf_op jit(solution)/shard_map/mul | solution.py:225
  883.3 13.0 fusion.71
  896.3 17.5 %multiply_reduce_fusion = (f32[12,512]{1,0:T(8,128)}, f32[12,512,1024]{2,1,0:T(8,128)}) fusion(f32[12,512,1024]{2,1,0:T(8,128)} %get-tuple-element.87, f32[12,512]{1,0:T(8,128)} %log_add_fusion, bf16[512,12,64]{0,2,1:T(8,128)(2,1)} %bitcast.132, bf16[1024,12,64]{0,2,1:T(8,128)(2,1)} %bitcast.136), kind=kOutput, calls=%fused_computation.7 | convolution fusion | flops 824174592 | bytes 52740096 | tf_op jit(solution)/shard_map/qhd,khd->hqk/dot_general | solution.py:222
  913.7 25.8 %subtract_multiply_fusion = f32[12,512,1024]{2,1,0:T(8,128)} fusion(f32[12,512,1024]{2,1,0:T(8,128)} %get-tuple-element.96, f32[12,512,1024]{2,1,0:T(8,128)} %get-tuple-element.87, f32[12,512]{1,0:T(8,128)} %get-tuple-element.95, f32[12,512]{1,0:T(8,128)} %log_add_fusion), kind=kLoop, calls=%fused_computation.6 | loop fusion | flops 18874368 | bytes 75546624 | tf_op jit(solution)/shard_map/mul | solution.py:225
  939.6 13.0 fusion.68
  1012.2 22.9 %pad.21 = f32[12,512,1534]{2,1,0:T(8,128)} pad(f32[12,512,1024]{2,1,0:T(8,128)} %subtract_multiply_fusion.1, f32[]{:T(128)} %constant.82.clone.1), padding=0_0x0_0x0_510 | pad | bytes 62865412 | tf_op jit(solution)/shard_map/jit(_pad)/pad | solution.py:45
  1035.1 22.9 %pad.23 = f32[12,512,1534]{2,1,0:T(8,128)} pad(f32[12,512,1024]{2,1,0:T(8,128)} %subtract_multiply_fusion, f32[]{:T(128)} %constant.82.clone.1), padding=0_0x0_0x0_510 | pad | bytes 62865412 | tf_op jit(solution)/shard_map/jit(_pad)/pad | solution.py:45
  1073.6 70.1 %reshape.244 = f32[12,785408]{1,0:T(8,128)} reshape(f32[12,512,1534]{2,1,0:T(8,128)} %pad.21) | data formatting | bytes 75399168 | tf_op jit(solution)/shard_map/reshape | solution.py:46
  1143.7 38.6 %pad.22 = f32[12,785920]{1,0:T(8,128)} pad(f32[12,785408]{1,0:T(8,128)} %reshape.244, f32[]{:T(128)} %constant.82.clone.1), padding=0_0x511_1 | pad | bytes 75423744 | tf_op jit(solution)/shard_map/jit(_pad)/pad | solution.py:47
  1182.3 91.8 %reshape.245 = f32[12,512,1535]{2,1,0:T(8,128)} reshape(f32[12,785920]{1,0:T(8,128)} %pad.22) | data formatting | bytes 75448320 | tf_op jit(solution)/shard_map/reshape | solution.py:48
  1274.2 13.8 reduce_sum.159
  1288.0 69.0 %reshape.246 = f32[12,785408]{1,0:T(8,128)} reshape(f32[12,512,1534]{2,1,0:T(8,128)} %pad.23) | data formatting | bytes 75399168 | tf_op jit(solution)/shard_map/reshape | solution.py:46
  1357.0 37.7 %pad.24 = f32[12,785920]{1,0:T(8,128)} pad(f32[12,785408]{1,0:T(8,128)} %reshape.246, f32[]{:T(128)} %constant.82.clone.1), padding=0_0x511_1 | pad | bytes 75423744 | tf_op jit(solution)/shard_map/jit(_pad)/pad | solution.py:47
  1394.7 77.0 %reshape.247 = f32[12,512,1535]{2,1,0:T(8,128)} reshape(f32[12,785920]{1,0:T(8,128)} %pad.24) | data formatting | bytes 75448320 | tf_op jit(solution)/shard_map/reshape | solution.py:48
  1471.7 13.8 reduce_sum.160
  1487.6 39.0 %all-reduce.7 = (f32[32,12]{0,1:T(8,128)}, f32[768]{0:T(1024)}, f32[768]{0:T(1024)}, f32[768,8]{0,1:T(8,128)}) all-reduce(f32[32,12]{0,1:T(8,128)S(1)} %fusion.76, f32[768]{0:T(1024)S(1)} %copy-done.61, f32[768]{0:T(1024)S(1)} %copy-done.60, f32[768,8]{0,1:T(8,128)S(1)} %copy-done.49), channel_id=1, replica_groups=mesh['dp'=4,'expert'=8] {'dp','expert'}, use_global_device_ids=true, to_apply=%region_26.27 | all-reduce | flops 8064 | bytes 64512 | tf_op jit(solution)/shard_map/psum | solution.py:264
  (240 shorter events, 289.8 us)
Async XLA Ops:
  8.0 17.4 %copy-start = (bf16[768,768]{1,0:T(8,128)(2,1)S(1)}, bf16[768,768]{1,0:T(8,128)(2,1)}, u32[]{:S(2)}) copy-start(bf16[768,768]{1,0:T(8,128)(2,1)} %param.22) | copy-start | bytes 3538948
  343.6 86.1 %copy-start.3 = (bf16[1024,768]{0,1:T(8,128)(2,1)S(1)}, bf16[1024,768]{0,1:T(8,128)(2,1)}, u32[]{:S(2)}) copy-start(bf16[1024,768]{0,1:T(8,128)(2,1)} %convolution_convert_fusion.1) | copy-start | bytes 4718596
  343.6 86.1 %copy-start.21 = (bf16[512,768]{0,1:T(8,128)(2,1)S(1)}, bf16[512,768]{0,1:T(8,128)(2,1)}, u32[]{:S(2)}) copy-start(bf16[512,768]{0,1:T(8,128)(2,1)} %get-tuple-element.78) | copy-start | bytes 2359300
  446.5 11.1 copy-start.23
  446.5 11.1 copy-start.43
  457.6 11.4 copy-start.47
  457.6 11.4 copy-start.18
  485.9 11.1 copy-start.24
  485.9 11.1 copy-start.45
  497.0 10.5 copy-start.40
  513.5 95.9 %copy-start.5 = (bf16[1024,768]{0,1:T(8,128)(2,1)}, bf16[1024,768]{0,1:T(8,128)(2,1)S(1)}, u32[]{:S(2)}) copy-start(bf16[1024,768]{0,1:T(8,128)(2,1)S(1)} %multiply_convert_fusion.1) | copy-start | bytes 4718596
  522.8 69.1 %slice-start.1 = ((s8[4718592]{0:T(1024)(128)(4,1)}), s8[4194304]{0:T(1024)(128)(4,1)S(1)}, s32[]{:S(2)}) async-start(s8[4718592]{0:T(1024)(128)(4,1)} %bitcast.158), calls=%async_computation.10 | async-start | bytes 8388608
  578.1 13.8 slice-start.2
  602.3 50.7 %all-to-all-start.1 = ((bf16[8,160,768]{2,1,0:T(8,128)(2,1)}), bf16[8,160,768]{2,1,0:T(8,128)(2,1)}, u32[]{:S(2)}, u32[]{:S(2)}) async-start(bf16[8,160,768]{2,1,0:T(8,128)(2,1)} %fusion.53), calls=%async_computation.1 | async-start | bytes 3932160 | tf_op jit(solution)/shard_map/all_to_all | solution.py:149
  606.8 919.8 %reduce-scatter.5.cloned.1.call-start = ((), (), s32[]{:S(2)}) async-start(), calls=%async_computation.7 | async-start | bytes 5898240 | tf_op jit(solution)/shard_map/reduce_scatter | solution.py:183
  609.7 217.1 %copy-start.38 = (f32[1024,8]{0,1:T(8,128)}, f32[1024,8]{0,1:T(8,128)S(1)}, u32[]{:S(2)}) copy-start(f32[1024,8]{0,1:T(8,128)S(1)} %get-tuple-element.93) | copy-start | bytes 98308
  766.6 49.9 %all-to-all-start.3 = ((bf16[8,160,768]{2,1,0:T(8,128)(2,1)}), bf16[8,160,768]{2,1,0:T(8,128)(2,1)S(1)}, u32[]{:S(2)}, u32[]{:S(2)}) async-start(bf16[8,160,768]{2,1,0:T(8,128)(2,1)} %fusion.50), calls=%async_computation.3 | async-start | bytes 3932160 | tf_op jit(solution)/shard_map/all_to_all | solution.py:174
  770.3 759.2 %reduce-scatter.3.cloned.1.call-start = ((), (), s32[]{:S(2)}) async-start(), calls=%async_computation.6 | async-start | bytes 5898240 | tf_op jit(solution)/shard_map/reduce_scatter | solution.py:180
  771.7 55.2 %copy-start.54 = (f32[1024]{0:T(1024)}, f32[1024]{0:T(1024)S(1)}, u32[]{:S(2)}) copy-start(f32[1024]{0:T(1024)S(1)} %mul.240) | copy-start | bytes 12292
  782.4 750.1 %all-reduce.11.cloned.1.call-start = ((), (), s32[]{:S(2)}) async-start(), calls=%async_computation.8 | async-start | bytes 18874368 | tf_op jit(solution)/shard_map/psum | solution.py:264
  857.4 25.9 %copy-start.4 = (bf16[1024,768]{0,1:T(8,128)(2,1)S(1)}, bf16[1024,768]{0,1:T(8,128)(2,1)}, u32[]{:S(2)}) copy-start(bf16[1024,768]{0,1:T(8,128)(2,1)} %convolution_convert_fusion.1) | copy-start | bytes 4718596
  954.2 24.7 %copy-start.35 = (bf16[1024,12,64]{0,2,1:T(8,128)(2,1)}, bf16[1024,12,64]{0,2,1:T(8,128)(2,1)S(1)}, u32[]{:S(2)}) copy-start(bf16[1024,12,64]{0,2,1:T(8,128)(2,1)S(1)} %pad_maximum_fusion.1) | copy-start | bytes 4718596
  954.2 10.9 copy-start.41
  965.1 11.0 copy-start.9
  965.1 11.0 copy-start.53
  965.1 11.0 copy-start.57
  981.8 10.5 copy-start.22
  1035.1 22.9 %copy-start.28 = (bf16[1024,768]{0,1:T(8,128)(2,1)S(1)}, bf16[1024,768]{0,1:T(8,128)(2,1)}, u32[]{:S(2)}) copy-start(bf16[1024,768]{0,1:T(8,128)(2,1)} %get-tuple-element.73) | copy-start | bytes 4718596
  1471.7 15.3 copy-start.67
  1471.7 15.9 %copy-start.49 = (f32[768,8]{0,1:T(8,128)S(1)}, f32[768,8]{0,1:T(8,128)}, u32[]{:S(2)}) copy-start(f32[768,8]{0,1:T(8,128)} %fusion.91) | copy-start | bytes 73732
  1471.7 15.8 %copy-start.60 = (f32[768]{0:T(1024)S(1)}, f32[768]{0:T(1024)}, u32[]{:S(2)}) copy-start(f32[768]{0:T(1024)} %get-tuple-element.60) | copy-start | bytes 9220
  1471.7 15.8 %copy-start.61 = (f32[768]{0:T(1024)S(1)}, f32[768]{0:T(1024)}, u32[]{:S(2)}) copy-start(f32[768]{0:T(1024)} %get-tuple-element.62) | copy-start | bytes 9220
  (46 other events, 142.3 us)
Sparse Core Ops, SparseCore 0:
  736.0 55.9 reduce-scatter.4
  795.3 57.0 reduce-scatter.2
Sparse Core Ops, SparseCore 1:
  1009.8 190.7 all-reduce.10
where the time goes:
time: 1560 us; the launch traced here: 1550 us
  local copies, waits for them, and re-layouts  912 us (58%)
  matrix products  269 us (17%)
  blocking collectives  140 us (9%)
  other arithmetic  127 us (8%)
  waiting for transfers between devices  77.3 us (5%)
  between operations  16.7 us (1%)
    reshape x2, local copies, waits for them, and re-layouts, bias_block(): return flat.reshape(head_count, block_rows, width - 1)[:, :, :seq_len]  176 us
    reshape x2, local copies, waits for them, and re-layouts, diagonal_sums(): return jnp.sum(flat.reshape(head_count, block_rows, width), axis=1)  169 us
    another operation x4, local copies, waits for them, and re-layouts, bias_block(): flat = jnp.tile(window, (1, block_rows))  149 us
    reshape x2, local copies, waits for them, and re-layouts, diagonal_sums(): flat = padded.reshape(head_count, block_rows * (width - 1))  139 us
    slice x2, local copies, waits for them, and re-layouts, bias_block(): flat = flat[:, block_rows - 1:block_rows - 1 + block_rows * (width - 1)]  76.5 us
    pad x2, local copies, waits for them, and re-layouts, diagonal_sums(): flat = jnp.pad(flat, ((0, 0), (block_rows - 1, 1)))  76.3 us
    all_to_all x1, blocking collectives, on_device(): lax.all_to_all(send_rows, 'expert', split_axis=0, concat_axis=0, tiled=True)  52.5 us
    mul x2, other arithmetic, on_device(): att_probs * (prob_grad - jnp.sum(att_probs * prob_grad, axis=-1, keepdims...  51.7 us
  transfers between devices with their start and end apart: 5, of which 2 were waited for; matrix products, arithmetic and copies ran while one was open for 46% of the time, Pallas kernels for 0%

commit v1 on v0

--- a/solution.py
+++ b/solution.py
@@ -262,17 +262,20 @@
         gain_two_grad,
         router_grad,
     ) = lax.psum(
-        (
-            query_w_grad,
-            key_w_grad,
-            value_w_grad,
-            out_w_grad,
-            rel_grad,
-            gain_one_grad,
-            gain_two_grad,
-            router_grad,
+        lax.psum(
+            (
+                query_w_grad,
+                key_w_grad,
+                value_w_grad,
+                out_w_grad,
+                rel_grad,
+                gain_one_grad,
+                gain_two_grad,
+                router_grad,
+            ),
+            "expert",
         ),
-        ("dp", "expert"),
+        "dp",
     )
     return (
         output,

time: 1560 us -> 1750 us (1.12)
  waiting for transfers between devices: 77.3 us -> 257 us
    psum x1, waiting for transfers between devices: 0.01 us -> 168 us  [on_device(): lax.psum((query_w_grad, key_w_grad, value_w_grad, out_w_grad, rel_grad, g...]
    psum x0 -> x1, blocking collectives: none -> 18.9 us  [on_device(): lax.psum(lax.psum((query_w_grad, key_w_grad, value_w_grad, out_w_grad, re...]
    unnamed x152 -> x176, local copies, waits for them, and re-layouts: 38.1 us -> 39.2 us
  transfers between devices with their start and end apart: 5 -> 6, of which waited for: 2 -> 3; matrix products, arithmetic and copies ran while one was open for 46% -> 29% of each run, Pallas kernels for 0% -> 0%
where the time goes in v1:
time: 1750 us; the launch traced here: 1740 us
  local copies, waits for them, and re-layouts  915 us (52%)
  matrix products  271 us (15%)
  waiting for transfers between devices  257 us (15%)
  blocking collectives  149 us (9%)
  other arithmetic  127 us (7%)
    reshape x2, local copies, waits for them, and re-layouts, bias_block(): return flat.reshape(head_count, block_rows, width - 1)[:, :, :seq_len]  176 us
    reshape x2, local copies, waits for them, and re-layouts, diagonal_sums(): return jnp.sum(flat.reshape(head_count, block_rows, width), axis=1)  169 us
    psum x1, waiting for transfers between devices, on_device(): lax.psum((query_w_grad, key_w_grad, value_w_grad, out_w_grad, rel_grad, g...  168 us
    another operation x4, local copies, waits for them, and re-layouts, bias_block(): flat = jnp.tile(window, (1, block_rows))  149 us
    reshape x2, local copies, waits for them, and re-layouts, diagonal_sums(): flat = padded.reshape(head_count, block_rows * (width - 1))  141 us
    pad x2, local copies, waits for them, and re-layouts, diagonal_sums(): flat = jnp.pad(flat, ((0, 0), (block_rows - 1, 1)))  77.1 us
    slice x2, local copies, waits for them, and re-layouts, bias_block(): flat = flat[:, block_rows - 1:block_rows - 1 + block_rows * (width - 1)]  76.5 us
    all_to_all x1, blocking collectives, on_device(): lax.all_to_all(send_rows, 'expert', split_axis=0, concat_axis=0, tiled=True)  52.5 us
  transfers between devices with their start and end apart: 6, of which 3 were waited for; matrix products, arithmetic and copies ran while one was open for 29% of the time, Pallas kernels for 0%

profile of v1, /device:TPU:0, one launch (start us, length us, event | category | flops | bytes accessed | tf_op | source)
XLA Modules:
  0.0 1743.7 jit_solution(8191858403802415426)
XLA Ops:
  40.7 61.7 %tile.9 = f32[12,785920]{1,0:T(8,128)} reshape(f32[12,512,1535]{2,1,0:T(8,128)} %tile.8) | data formatting | bytes 75448320 | tf_op jit(solution)/shard_map/tile | solution.py:37
  102.4 38.3 %slice.122 = f32[12,785408]{1,0:T(8,128)} slice(f32[12,785920]{1,0:T(8,128)} %tile.9), slice={[0:12], [511:785919]} | slice | bytes 75399168 | tf_op jit(solution)/shard_map/slice | solution.py:38
  140.7 90.3 %reshape.233 = f32[12,512,1534]{2,1,0:T(8,128)} reshape(f32[12,785408]{1,0:T(8,128)} %slice.122) | data formatting | bytes 75399168 | tf_op jit(solution)/shard_map/reshape | solution.py:39
  243.8 61.5 %tile.11 = f32[12,785920]{1,0:T(8,128)} reshape(f32[12,512,1535]{2,1,0:T(8,128)} %tile.10) | data formatting | bytes 75448320 | tf_op jit(solution)/shard_map/tile | solution.py:37
  305.3 38.3 %slice.126 = f32[12,785408]{1,0:T(8,128)} slice(f32[12,785920]{1,0:T(8,128)} %tile.11), slice={[0:12], [511:785919]} | slice | bytes 75399168 | tf_op jit(solution)/shard_map/slice | solution.py:38
  343.5 86.1 %reshape.234 = f32[12,512,1534]{2,1,0:T(8,128)} reshape(f32[12,785408]{1,0:T(8,128)} %slice.126) | data formatting | bytes 75399168 | tf_op jit(solution)/shard_map/reshape | solution.py:39
  429.6 16.9 fusion.105
  469.0 16.8 fusion.104
  524.1 52.5 %all_to_all.20 = bf16[8,160,768]{2,1,0:T(8,128)(2,1)S(1)} all-to-all(bf16[8,160,768]{2,1,0:T(8,128)(2,1)S(1)} %bitcast.125), channel_id=1, replica_groups=mesh['dp'=4,'expert'=8] {'expert'}, dimensions={0} | all-to-all | bytes 3932160 | tf_op jit(solution)/shard_map/all_to_all | solution.py:140
  609.9 43.2 %all-to-all-done.1 = bf16[8,160,768]{2,1,0:T(8,128)(2,1)} async-done(((bf16[8,160,768]{2,1,0:T(8,128)(2,1)}), bf16[8,160,768]{2,1,0:T(8,128)(2,1)}, u32[]{:S(2)}, u32[]{:S(2)}) %all-to-all-start.1) | async-done | bytes 1966112 | tf_op jit(solution)/shard_map/all_to_all | solution.py:149
  675.1 48.9 %all_to_all.21 = bf16[8,160,768]{2,1,0:T(8,128)(2,1)S(1)} all-to-all(bf16[8,160,768]{2,1,0:T(8,128)(2,1)S(1)} %bitcast.127), channel_id=1, replica_groups=mesh['dp'=4,'expert'=8] {'expert'}, dimensions={0} | all-to-all | bytes 3932160 | tf_op jit(solution)/shard_map/all_to_all | solution.py:163
  724.1 18.3 %fusion.10 = bf16[8,160,3072]{2,1,0:T(8,128)(2,1)S(1)} fusion(f32[8,160,3072]{2,1,0:T(8,128)} %copy-done.78, bf16[8,160,768]{2,1,0:T(8,128)(2,1)S(1)} %all_to_all.21, bf16[1,3072,768]{2,1,0:T(8,128)(2,1)} %param.28), kind=kOutput, calls=%fused_computation.28 | convolution fusion | flops 6118440960 | bytes 30277632 | tf_op jit(solution)/shard_map/scd,fd->scf/dot_general | solution.py:167
  758.1 44.9 %all-to-all-done.3 = bf16[8,160,768]{2,1,0:T(8,128)(2,1)S(1)} async-done(((bf16[8,160,768]{2,1,0:T(8,128)(2,1)}), bf16[8,160,768]{2,1,0:T(8,128)(2,1)S(1)}, u32[]{:S(2)}, u32[]{:S(2)}) %all-to-all-start.3) | async-done | bytes 1966112 | tf_op jit(solution)/shard_map/all_to_all | solution.py:174
  836.7 20.3 %multiply_reduce_fusion = (f32[12,512]{1,0:T(8,128)}, f32[12,512,1024]{2,1,0:T(8,128)}) fusion(f32[12,512,1024]{2,1,0:T(8,128)} %get-tuple-element.95, f32[12,512]{1,0:T(8,128)} %log_add_fusion, bf16[512,12,64]{0,2,1:T(8,128)(2,1)S(1)} %bitcast.133, bf16[1024,12,64]{0,2,1:T(8,128)(2,1)S(1)} %bitcast.139), kind=kOutput, calls=%fused_computation.7 | convolution fusion | flops 824174592 | bytes 52740096 | tf_op jit(solution)/shard_map/qhd,khd->hqk/dot_general | solution.py:222
  857.0 26.1 %subtract_multiply_fusion = f32[12,512,1024]{2,1,0:T(8,128)} fusion(f32[12,512,1024]{2,1,0:T(8,128)} %get-tuple-element.104, f32[12,512,1024]{2,1,0:T(8,128)} %get-tuple-element.95, f32[12,512]{1,0:T(8,128)} %get-tuple-element.103, f32[12,512]{1,0:T(8,128)} %log_add_fusion), kind=kLoop, calls=%fused_computation.6 | loop fusion | flops 18874368 | bytes 75546624 | tf_op jit(solution)/shard_map/mul | solution.py:225
  883.1 13.0 fusion.68
  908.3 17.2 multiply_reduce_fusion.1
  940.1 26.0 %subtract_multiply_fusion.1 = f32[12,512,1024]{2,1,0:T(8,128)} fusion(f32[12,512,1024]{2,1,0:T(8,128)} %get-tuple-element.106, f32[12,512,1024]{2,1,0:T(8,128)} %get-tuple-element.97, f32[12,512]{1,0:T(8,128)S(1)} %copy-done.53, f32[12,512]{1,0:T(8,128)S(1)} %copy-done.46), kind=kLoop, calls=%fused_computation.9 | loop fusion | flops 18874368 | bytes 75546624 | tf_op jit(solution)/shard_map/mul | solution.py:225
  966.1 13.0 fusion.71
  1024.3 168.4 %all-reduce.14.cloned.1.call-done = (f32[768,768]{1,0:T(8,128)}, f32[768,768]{1,0:T(8,128)}, f32[768,768]{1,0:T(8,128)}, f32[768,768]{1,0:T(8,128)}) async-done(((f32[768,768]{1,0:T(8,128)}, f32[768,768]{1,0:T(8,128)}, f32[768,768]{1,0:T(8,128)}, f32[768,768]{1,0:T(8,128)}), (f32[768,768]{1,0:T(8,128)}, f32[768,768]{1,0:T(8,128)}, f32[768,768]{1,0:T(8,128)}, ...) | async-done | bytes 9437200 | tf_op jit(solution)/shard_map/psum | solution.py:265
  1195.3 22.3 %pad.21 = f32[12,512,1534]{2,1,0:T(8,128)} pad(f32[12,512,1024]{2,1,0:T(8,128)} %subtract_multiply_fusion.1, f32[]{:T(128)} %constant.82.clone.1), padding=0_0x0_0x0_510 | pad | bytes 62865412 | tf_op jit(solution)/shard_map/jit(_pad)/pad | solution.py:45
  1217.6 23.4 %pad.23 = f32[12,512,1534]{2,1,0:T(8,128)} pad(f32[12,512,1024]{2,1,0:T(8,128)} %subtract_multiply_fusion, f32[]{:T(128)} %constant.82.clone.1), padding=0_0x0_0x0_510 | pad | bytes 62865412 | tf_op jit(solution)/shard_map/jit(_pad)/pad | solution.py:45
  1256.5 71.9 %reshape.244 = f32[12,785408]{1,0:T(8,128)} reshape(f32[12,512,1534]{2,1,0:T(8,128)} %pad.21) | data formatting | bytes 75399168 | tf_op jit(solution)/shard_map/reshape | solution.py:46
  1328.4 39.4 %pad.22 = f32[12,785920]{1,0:T(8,128)} pad(f32[12,785408]{1,0:T(8,128)} %reshape.244, f32[]{:T(128)} %constant.82.clone.1), padding=0_0x511_1 | pad | bytes 75423744 | tf_op jit(solution)/shard_map/jit(_pad)/pad | solution.py:47
  1367.8 91.8 %reshape.245 = f32[12,512,1535]{2,1,0:T(8,128)} reshape(f32[12,785920]{1,0:T(8,128)} %pad.22) | data formatting | bytes 75448320 | tf_op jit(solution)/shard_map/reshape | solution.py:48
  1459.6 13.8 reduce_sum.159
  1473.4 69.1 %reshape.246 = f32[12,785408]{1,0:T(8,128)} reshape(f32[12,512,1534]{2,1,0:T(8,128)} %pad.23) | data formatting | bytes 75399168 | tf_op jit(solution)/shard_map/reshape | solution.py:46
  1542.5 37.7 %pad.24 = f32[12,785920]{1,0:T(8,128)} pad(f32[12,785408]{1,0:T(8,128)} %reshape.246, f32[]{:T(128)} %constant.82.clone.1), padding=0_0x511_1 | pad | bytes 75423744 | tf_op jit(solution)/shard_map/jit(_pad)/pad | solution.py:47
  1580.1 76.9 %reshape.247 = f32[12,512,1535]{2,1,0:T(8,128)} reshape(f32[12,785920]{1,0:T(8,128)} %pad.24) | data formatting | bytes 75448320 | tf_op jit(solution)/shard_map/reshape | solution.py:48
  1657.1 13.8 reduce_sum.160
  1672.9 28.2 %all-reduce.7 = (f32[32,12]{0,1:T(8,128)S(1)}, f32[768]{0:T(1024)S(1)}, f32[768]{0:T(1024)S(1)}, f32[768,8]{0,1:T(8,128)S(1)}) all-reduce(f32[32,12]{0,1:T(8,128)S(1)} %fusion.76, f32[768]{0:T(1024)S(1)} %copy-done.71, f32[768]{0:T(1024)S(1)} %copy-done.70, f32[768,8]{0,1:T(8,128)S(1)} %copy-done.58), channel_id=1, replica_groups=mesh['dp'=4,'expert'=8] {'expert'}, use_global_device_ids=true, to_apply=%region_30.31 | all-reduce | flops 8064 | bytes 64512 | tf_op jit(solution)/shard_map/psum | solution.py:265
  1701.2 18.9 %all-reduce.9 = (f32[32,12]{0,1:T(8,128)}, f32[768]{0:T(1024)}, f32[768]{0:T(1024)}, f32[768,8]{0,1:T(8,128)}) all-reduce(f32[32,12]{0,1:T(8,128)S(1)} %get-tuple-element.64, f32[768]{0:T(1024)S(1)} %get-tuple-element.65, f32[768]{0:T(1024)S(1)} %get-tuple-element.66, ...), channel_id=1, replica_groups=mesh['dp'=4,'expert'=8] {'dp'}, use_global_device_ids=true, to_apply=%region_31.32 | all-reduce | flops 8064 | bytes 64512 | tf_op jit(solution)/shard_map/psum | solution.py:264
  (269 shorter events, 317.9 us)
Async XLA Ops:
  8.0 17.4 copy-start
  343.5 86.1 %copy-start.3 = (bf16[1024,768]{0,1:T(8,128)(2,1)S(1)}, bf16[1024,768]{0,1:T(8,128)(2,1)}, u32[]{:S(2)}) copy-start(bf16[1024,768]{0,1:T(8,128)(2,1)} %convolution_convert_fusion.1) | copy-start | bytes 4718596
  343.5 86.1 %copy-start.22 = (bf16[512,768]{0,1:T(8,128)(2,1)S(1)}, bf16[512,768]{0,1:T(8,128)(2,1)}, u32[]{:S(2)}) copy-start(bf16[512,768]{0,1:T(8,128)(2,1)} %get-tuple-element.86) | copy-start | bytes 2359300
  513.4 96.1 %copy-start.5 = (bf16[1024,768]{0,1:T(8,128)(2,1)}, bf16[1024,768]{0,1:T(8,128)(2,1)S(1)}, u32[]{:S(2)}) copy-start(bf16[1024,768]{0,1:T(8,128)(2,1)S(1)} %multiply_convert_fusion.1) | copy-start | bytes 4718596
  522.5 69.1 %slice-start.1 = ((s8[4718592]{0:T(1024)(128)(4,1)}), s8[4194304]{0:T(1024)(128)(4,1)S(1)}, s32[]{:S(2)}) async-start(s8[4718592]{0:T(1024)(128)(4,1)} %bitcast.158), calls=%async_computation.11 | async-start | bytes 8388608
  577.9 13.8 slice-start.2
  602.0 51.1 %all-to-all-start.1 = ((bf16[8,160,768]{2,1,0:T(8,128)(2,1)}), bf16[8,160,768]{2,1,0:T(8,128)(2,1)}, u32[]{:S(2)}, u32[]{:S(2)}) async-start(bf16[8,160,768]{2,1,0:T(8,128)(2,1)} %fusion.53), calls=%async_computation.1 | async-start | bytes 3932160 | tf_op jit(solution)/shard_map/all_to_all | solution.py:149
  609.8 203.0 %copy-start.43 = (f32[1024,8]{0,1:T(8,128)}, f32[1024,8]{0,1:T(8,128)S(1)}, u32[]{:S(2)}) copy-start(f32[1024,8]{0,1:T(8,128)S(1)} %get-tuple-element.101) | copy-start | bytes 98308
  609.8 203.0 %copy-start.56 = (f32[1024]{0:T(1024)}, f32[1024]{0:T(1024)S(1)}, u32[]{:S(2)}) copy-start(f32[1024]{0:T(1024)S(1)} %get-tuple-element.100) | copy-start | bytes 12292
  609.9 203.0 %copy-start.59 = (f32[1024]{0:T(1024)}, f32[1024]{0:T(1024)S(1)}, u32[]{:S(2)}) copy-start(f32[1024]{0:T(1024)S(1)} %fusion.90) | copy-start | bytes 12292
  675.0 70.4 %slice-start.3 = ((s8[4718592]{0:T(1024)(128)(4,1)}), s8[4194304]{0:T(1024)(128)(4,1)S(1)}, s32[]{:S(2)}) async-start(s8[4718592]{0:T(1024)(128)(4,1)} %bitcast.160), calls=%async_computation.13 | async-start | bytes 8388608
  724.1 18.3 %copy-start.36 = (bf16[8,160,768]{2,1,0:T(8,128)(2,1)}, bf16[8,160,768]{2,1,0:T(8,128)(2,1)S(1)}, u32[]{:S(2)}) copy-start(bf16[8,160,768]{2,1,0:T(8,128)(2,1)S(1)} %all_to_all.21) | copy-start | bytes 5898244
  724.1 21.3 %slice-start.4 = ((s8[4718592]{0:T(1024)(128)(4,1)}), s8[524288]{0:T(1024)(128)(4,1)S(1)}, s32[]{:S(2)}) async-start(s8[4718592]{0:T(1024)(128)(4,1)} %bitcast.160), calls=%async_computation.14 | async-start | bytes 1048576
  752.9 50.1 %all-to-all-start.3 = ((bf16[8,160,768]{2,1,0:T(8,128)(2,1)}), bf16[8,160,768]{2,1,0:T(8,128)(2,1)S(1)}, u32[]{:S(2)}, u32[]{:S(2)}) async-start(bf16[8,160,768]{2,1,0:T(8,128)(2,1)} %fusion.50), calls=%async_computation.3 | async-start | bytes 3932160 | tf_op jit(solution)/shard_map/all_to_all | solution.py:174
  756.8 435.9 %all-reduce.14.cloned.1.call-start = ((), (), s32[]{:S(2)}) async-start(), calls=%async_computation.8 | async-start | bytes 18874368 | tf_op jit(solution)/shard_map/psum | solution.py:265
  758.1 54.8 %copy-start.65 = (f32[1024]{0:T(1024)}, f32[1024]{0:T(1024)S(1)}, u32[]{:S(2)}) copy-start(f32[1024]{0:T(1024)S(1)} %mul.240) | copy-start | bytes 12292
  824.7 12.0 copy-start.26
  857.0 26.1 %copy-start.4 = (bf16[1024,768]{0,1:T(8,128)(2,1)S(1)}, bf16[1024,768]{0,1:T(8,128)(2,1)}, u32[]{:S(2)}) copy-start(bf16[1024,768]{0,1:T(8,128)(2,1)} %convolution_convert_fusion.1) | copy-start | bytes 4718596
  883.1 13.0 copy-start.20
  908.3 17.2 copy-start.21
  925.5 11.7 copy-start.9
  925.5 11.7 copy-start.64
  925.5 11.7 copy-start.68
  966.1 13.1 copy-start.30
  997.2 722.8 %reduce-scatter.5.cloned.1.call-start = ((), (), s32[]{:S(2)}) async-start(), calls=%async_computation.7 | async-start | bytes 5898240 | tf_op jit(solution)/shard_map/reduce_scatter | solution.py:183
  1011.1 711.8 %reduce-scatter.3.cloned.1.call-start = ((), (), s32[]{:S(2)}) async-start(), calls=%async_computation.6 | async-start | bytes 5898240 | tf_op jit(solution)/shard_map/reduce_scatter | solution.py:180
  1024.2 701.7 %all-reduce.16.cloned.1.call-start = ((), (), s32[]{:S(2)}) async-start(), calls=%async_computation.9 | async-start | bytes 18874368 | tf_op jit(solution)/shard_map/psum | solution.py:264
  1217.6 23.4 %copy-start.29 = (bf16[1024,768]{0,1:T(8,128)(2,1)S(1)}, bf16[1024,768]{0,1:T(8,128)(2,1)}, u32[]{:S(2)}) copy-start(bf16[1024,768]{0,1:T(8,128)(2,1)} %get-tuple-element.81) | copy-start | bytes 4718596
  1657.1 15.2 copy-start.77
  1657.1 15.8 copy-start.58
  1657.1 15.8 copy-start.70
  1657.1 15.8 copy-start.71
  (59 other events, 232.1 us)
Sparse Core Ops, SparseCore 0:
  997.4 195.3 all-reduce.13
Sparse Core Ops, SparseCore 1:
  1011.2 55.5 reduce-scatter.4
  1069.7 56.9 reduce-scatter.2
  1192.9 189.9 all-reduce.15
